TPU v7x, 32 devices: a whole 2x2x4 slice. The times are simulated.
32 devices in a mesh: gx: 2 (over x), yz: 16 (over z, y, core).
Axes of the slice: x: 2, y: 2, z: 4, core: 2. Of those that a mesh axis runs over, the one named last changes fastest.
Arguments:
- displacement: float32 [3, 8, 16, 8, 256], P(None, 'gx', 'yz'), may hold values from -0.04 to 0.04
- velocity: float32 [3, 8, 16, 8, 256], P(None, 'gx', 'yz'), may hold values from -5 to 5
- rest_length: float32 [18, 8, 16, 8, 256], P(None, 'gx', 'yz'), may hold values from 0.96 to 1.48, as said below
- heights: int32 [8, 32], replicated, may hold values from 512 to 1024
Outputs:
- new_displacement: float32 [3, 8, 16, 8, 256], P(None, 'gx', 'yz')
- half_velocity: float32 [3, 8, 16, 8, 256], P(None, 'gx', 'yz')
- boost_factor: float32 [], replicated
Inputs may be any that keep to these rules, and one draw needn't show every extreme that they name: rest_length[k + 9] of an atom equals rest_length[k] of the atom -d_k away from it, wherever both atoms lie within the layers.
All inputs are finite; a program needn't handle non-finite values.
Results may differ from a plain program's by a relative error of at most 0.0003.
Values sent between devices are 32-bit elements; how exact they have to be, the bound alone decides.
A program may use at most 128 MiB of HBM per device.

v0:
```python
import jax
import jax.numpy as jnp
from jax import lax
from jax.sharding import PartitionSpec as P

ZT = 4


CUTOFF = 1.5
REACH_RADIUS = 3.5
DENSITY_DECAY = 3.0
PAIR_DECAY = 6.0
PAIR_SCALE = 0.6
EMBED_SCALE = 1.0
DENSITY_FLOOR = 0.5
SHARPNESS = 8.0
STRAIN_LIMIT = 0.1
BIAS_SCALE = 0.08
KICK_FACTOR = 0.2
TIME_STEP = 0.05
THERMAL = 0.5


def from_behind(x, axis, by):
    size = lax.axis_size(axis)
    return lax.ppermute(x, axis, [(i, (i + by) % size) for i in range(size)])


def list_offsets(reach_sq, forward_only):
    chosen = []
    for along_x in range(-3, 4):
        for along_y in range(-3, 4):
            for along_z in range(-3, 4):
                length_sq = along_x * along_x + along_y * along_y + along_z * along_z
                if 0 < length_sq <= reach_sq:
                    if not forward_only or (along_x, along_y, along_z) > (0, 0, 0):
                        chosen.append((along_x, along_y, along_z))
    return chosen


def bond_offsets():
    forward = list_offsets(2, True)
    return forward + [(-vector[0], -vector[1], -vector[2]) for vector in forward]


def taper_value(radius, cutoff):
    inside = 1.0 - (radius / cutoff) ** 2
    return jnp.where(radius < cutoff, inside * inside, 0.0)


def taper_slope(radius, cutoff):
    inside = 1.0 - (radius / cutoff) ** 2
    return jnp.where(radius < cutoff, -4.0 * radius * inside / (cutoff * cutoff), 0.0)


def across_x(outgoing, distance):
    return from_behind(outgoing, "gx", distance)


def across_y(outgoing, distance):
    return from_behind(outgoing, "yz", distance)


def across_z(outgoing, distance):
    return from_behind(outgoing, "yz", distance)


def add_ghosts(quantity, rim_width, z_tile):
    lower_rim = across_x(quantity[:, -rim_width:], 1)
    upper_rim = across_x(quantity[:, :rim_width], -1)
    quantity = jnp.concatenate([lower_rim, quantity, upper_rim], axis=1)
    lower_rim = across_y(quantity[:, :, -rim_width:], ZT)
    upper_rim = across_y(quantity[:, :, :rim_width], -ZT)
    quantity = jnp.concatenate([lower_rim, quantity, upper_rim], axis=2)
    lower_rim = across_z(quantity[..., -rim_width:], 1)
    upper_rim = across_z(quantity[..., :rim_width], -1)
    lower_rim = jnp.where(z_tile > 0, lower_rim, jnp.zeros_like(lower_rim))
    upper_rim = jnp.where(z_tile < ZT - 1, upper_rim, jnp.zeros_like(upper_rim))
    return jnp.concatenate([lower_rim, quantity, upper_rim], axis=3)


def window(source, offset, corner, extent):
    return source[
        ...,
        corner + offset[0] : corner + offset[0] + extent[0],
        corner + offset[1] : corner + offset[1] + extent[1],
        corner + offset[2] : corner + offset[2] + extent[2],
    ]


def separation(padded_positions, offset, corner, extent):
    center = window(padded_positions, (0, 0, 0), corner, extent)
    beside = window(padded_positions, offset, corner, extent)
    pieces = [offset[component] + beside[component] - center[component] for component in range(3)]
    radius = jnp.sqrt(pieces[0] * pieces[0] + pieces[1] * pieces[1] + pieces[2] * pieces[2])
    return (pieces, radius)


def presence(heights, margin, x_tile, y_tile, z_tile, extent):
    wrapped = jnp.pad(heights, margin, mode="wrap")
    local_heights = lax.dynamic_slice(
        wrapped,
        (x_tile * extent[0], y_tile * extent[1]),
        (extent[0] + 2 * margin, extent[1] + 2 * margin),
    )
    layer_index = (
        z_tile * extent[2]
        - margin
        + lax.broadcasted_iota(jnp.int32, (1, 1, extent[2] + 2 * margin), 2)
    )
    return ((layer_index >= 0) & (layer_index < local_heights[:, :, None])).astype(jnp.float32)


def reach_forces(
    padded_positions,
    margin,
    padded_adjoint,
    adjoint_margin,
    padded_embed,
    adjoint_total,
    bond_energy,
    extent,
):
    forces = [jnp.zeros(adjoint_total.shape, jnp.float32) for component in range(3)]
    adjoint_lambda = adjoint_total
    for offset in list_offsets(9, False):
        pieces, radius = separation(padded_positions, offset, margin, extent)
        far_adjoint = window(padded_adjoint[0], offset, adjoint_margin, extent)
        far_energy = window(padded_embed[1], offset, 3, extent)
        weight = (
            (adjoint_total * far_energy + far_adjoint * bond_energy)
            * taper_slope(radius, REACH_RADIUS)
            / radius
        )
        forces = [forces[component] + weight * pieces[component] for component in range(3)]
        adjoint_lambda = adjoint_lambda + taper_value(radius, REACH_RADIUS) * far_adjoint
    return (forces, adjoint_lambda)


def body(displacement, velocity, rest_length, heights):
    own_positions = displacement[:, :, 0]
    own_velocity = velocity[:, :, 0]
    rest_bonds = rest_length[:, :, 0]
    extent = (own_positions.shape[1], own_positions.shape[2], own_positions.shape[3])
    tiles_along_y = lax.axis_size("yz") // ZT
    x_tile = lax.axis_index("gx")
    shifted_index = lax.axis_index("yz") + ZT // 2
    y_tile = shifted_index // ZT % tiles_along_y
    z_tile = shifted_index % ZT
    margin = 3
    padded_positions = add_ghosts(own_positions, margin, z_tile)
    present = presence(heights, margin, x_tile, y_tile, z_tile, extent)
    own_present = window(present, (0, 0, 0), margin, extent)
    bond_list = bond_offsets()
    density = jnp.zeros(own_present.shape, jnp.float32)
    bond_energy = jnp.zeros(own_present.shape, jnp.float32)
    bond_room = jnp.zeros(own_present.shape, jnp.float32)
    for bond_index in range(18):
        offset = bond_list[bond_index]
        pieces, radius = separation(padded_positions, offset, margin, extent)
        partner = window(present, offset, margin, extent)
        paired = own_present * partner
        density = density + partner * jnp.exp(-DENSITY_DECAY * (radius - 1.0)) * taper_value(
            radius, CUTOFF
        )
        relative = (radius - rest_bonds[bond_index]) / (rest_bonds[bond_index] * STRAIN_LIMIT)
        squared = relative * relative
        bond_energy = bond_energy + paired * jnp.exp(SHARPNESS * squared)
        bond_room = bond_room + paired * (1.0 - squared)
    embed_slope = -0.5 * EMBED_SCALE / jnp.sqrt(density + DENSITY_FLOOR)
    padded_embed = add_ghosts(jnp.stack([embed_slope, bond_energy]), 3, z_tile)
    smooth_total = 1.0 + bond_energy
    for offset in list_offsets(9, False):
        pieces, radius = separation(padded_positions, offset, margin, extent)
        smooth_total = smooth_total + taper_value(radius, REACH_RADIUS) * window(
            padded_embed[1], offset, 3, extent
        )
    smooth_max = jnp.log(smooth_total) / SHARPNESS
    bias_gain = BIAS_SCALE / (1.0 + smooth_max * smooth_max)
    bias_energy = own_present * bias_gain * bond_room
    adjoint_total = (
        own_present
        * bond_room
        * BIAS_SCALE
        * (-2.0 * smooth_max)
        / (1.0 + smooth_max * smooth_max) ** 2
        / (SHARPNESS * smooth_total)
    )
    adjoint_pair = jnp.stack([adjoint_total, bias_gain])
    adjoint_margin = 3
    padded_adjoint = add_ghosts(adjoint_pair, 3, z_tile)
    forces, adjoint_lambda = reach_forces(
        padded_positions,
        margin,
        padded_adjoint,
        adjoint_margin,
        padded_embed,
        adjoint_total,
        bond_energy,
        extent,
    )
    padded_lambda = add_ghosts(adjoint_lambda[None], 1, z_tile)[0]
    own_lambda = window(padded_lambda, (0, 0, 0), 1, extent)
    for bond_index in range(18):
        offset = bond_list[bond_index]
        pieces, radius = separation(padded_positions, offset, margin, extent)
        paired = own_present * window(present, offset, margin, extent)
        cut_value = taper_value(radius, CUTOFF)
        cut_slope = taper_slope(radius, CUTOFF)
        density_slope = jnp.exp(-DENSITY_DECAY * (radius - 1.0)) * (
            cut_slope - DENSITY_DECAY * cut_value
        )
        pair_slope = (
            PAIR_SCALE
            * jnp.exp(-PAIR_DECAY * (radius - 1.0))
            * (cut_slope - PAIR_DECAY * cut_value)
        )
        relative = (radius - rest_bonds[bond_index]) / (rest_bonds[bond_index] * STRAIN_LIMIT)
        squared = relative * relative
        lifted = jnp.exp(SHARPNESS * squared)
        strain_slope = 2.0 * relative / (rest_bonds[bond_index] * STRAIN_LIMIT)
        far_slope = window(padded_embed[0], offset, 3, extent)
        far_gain = window(padded_adjoint[1], offset, adjoint_margin, extent)
        far_lambda = window(padded_lambda, offset, 1, extent)
        coupled = paired * (
            pair_slope
            + (embed_slope + far_slope) * density_slope
            + (SHARPNESS * (own_lambda + far_lambda) * lifted - bias_gain - far_gain) * strain_slope
        )
        weight = coupled / radius
        forces = [forces[component] + weight * pieces[component] for component in range(3)]
    half_velocity = own_velocity + KICK_FACTOR * jnp.stack(forces)
    new_displacement = own_positions + TIME_STEP * half_velocity
    totals = lax.psum(
        (jnp.sum(own_present * jnp.exp(bias_energy / THERMAL)), jnp.sum(own_present)), ("gx", "yz")
    )
    boost_factor = totals[0] / totals[1]
    return (new_displacement[:, :, None], half_velocity[:, :, None], boost_factor)


def solution(mesh):
    in_specs = (
        P(None, "gx", "yz", None, None),
        P(None, "gx", "yz", None, None),
        P(None, "gx", "yz", None, None),
        P(),
    )
    out_specs = (P(None, "gx", "yz", None, None), P(None, "gx", "yz", None, None), P())
    return jax.shard_map(body, mesh=mesh, in_specs=in_specs, out_specs=out_specs, check_vma=False)
```

profile of v0, /device:TPU:0, one launch (start us, length us, event | category | flops | bytes accessed | tf_op | source)
XLA Modules:
  0.0 215.7 jit_solution(17456053623484448128)
XLA Ops:
  1.6 3.0 %collective-permute-start = (f32[3,3,8,256]{3,2,1,0:T(8,128)S(1)}, f32[3,3,8,256]{3,2,1,0:T(8,128)S(1)}, u32[]{:S(2)}, u32[]{:S(2)}) collective-permute-start(f32[3,3,8,256]{3,2,1,0:T(8,128)S(1)} %get-tuple-element.833), channel_id=1, source_target_pairs={{0,16},{16,0},{1,17},{17,1},{2,18},{18,2},{3,19},{19,3},{4,20},{20... | collective-permute-start | bytes 221192 | tf_op jit(solution)/shard_map/ppermute | solution.py:26
  7.2 1.8 collective-permute-done.1
  10.8 2.2 %collective-permute-start.3 = (f32[3,10,3,256]{3,2,1,0:T(4,128)S(1)}, f32[3,10,3,256]{3,2,1,0:T(4,128)S(1)}, u32[]{:S(2)}, u32[]{:S(2)}) collective-permute-start(f32[3,10,3,256]{3,2,1,0:T(4,128)S(1)} %get-tuple-element.820), channel_id=1, source_target_pairs={{0,12},{1,13},{2,14},{3,15},{4,0},{5,1},{6,2},{7,3},{8,4},{9,5},{1... | collective-permute-start | bytes 276488 | tf_op jit(solution)/shard_map/ppermute | solution.py:26
  13.6 3.4 %collective-permute-done.2 = f32[3,10,3,256]{3,2,1,0:T(4,128)S(1)} collective-permute-done((f32[3,10,3,256]{3,2,1,0:T(4,128)S(1)}, f32[3,10,3,256]{3,2,1,0:T(4,128)S(1)}, u32[]{:S(2)}, u32[]{:S(2)}) %collective-permute-start.2) | collective-permute-done | bytes 92192 | tf_op jit(solution)/shard_map/ppermute | solution.py:26
  23.3 2.1 collective-permute-start.4
  26.1 3.0 %collective-permute-done.4 = f32[3,10,14,3]{3,2,1,0:T(8,128)S(1)} collective-permute-done((f32[3,10,14,3]{3,2,1,0:T(8,128)S(1)}, f32[3,10,14,3]{3,2,1,0:T(8,128)S(1)}, u32[]{:S(2)}, u32[]{:S(2)}) %collective-permute-start.4) | collective-permute-done | bytes 5072 | tf_op jit(solution)/shard_map/ppermute | solution.py:26
  29.2 5.3 %collective-permute-done.5 = f32[3,10,14,3]{3,2,1,0:T(8,128)S(1)} collective-permute-done((f32[3,10,14,3]{3,2,1,0:T(8,128)S(1)}, f32[3,10,14,3]{3,2,1,0:T(8,128)S(1)}, u32[]{:S(2)}, u32[]{:S(2)}) %collective-permute-start.5) | collective-permute-done | bytes 5072 | tf_op jit(solution)/shard_map/ppermute | solution.py:26
  60.8 1.9 rsqrt_multiply_fusion
  68.3 3.8 %collective-permute-start.9 = (f32[2,10,3,256]{3,2,1,0:T(4,128)S(1)}, f32[2,10,3,256]{3,2,1,0:T(4,128)S(1)}, u32[]{:S(2)}, u32[]{:S(2)}) collective-permute-start(f32[2,10,3,256]{3,2,1,0:T(4,128)S(1)} %get-tuple-element.824), channel_id=1, source_target_pairs={{0,12},{1,13},{2,14},{3,15},{4,0},{5,1},{6,2},{7,3},{8,4},{9,5},{1... | collective-permute-start | bytes 184328 | tf_op jit(solution)/shard_map/ppermute | solution.py:26
  75.6 4.4 %collective-permute-start.11 = (f32[2,10,14,3]{3,2,1,0:T(8,128)S(1)}, f32[2,10,14,3]{3,2,1,0:T(8,128)S(1)}, u32[]{:S(2)}, u32[]{:S(2)}) collective-permute-start(f32[2,10,14,3]{3,2,1,0:T(8,128)S(1)} %get-tuple-element.815), channel_id=1, source_target_pairs={{0,15},{1,0},{2,1},{3,2},{4,3},{5,4},{6,5},{7,6},{8,7},{9,8},{10,9... | collective-permute-start | bytes 10088 | tf_op jit(solution)/shard_map/ppermute | solution.py:26
  80.0 2.2 %collective-permute-done.10 = f32[2,10,14,3]{3,2,1,0:T(8,128)S(1)} collective-permute-done((f32[2,10,14,3]{3,2,1,0:T(8,128)S(1)}, f32[2,10,14,3]{3,2,1,0:T(8,128)S(1)}, u32[]{:S(2)}, u32[]{:S(2)}) %collective-permute-start.10) | collective-permute-done | bytes 3392 | tf_op jit(solution)/shard_map/ppermute | solution.py:26
  84.4 7.4 %slice_reduce_fusion = (f32[]{:T(128)}, f32[]{:T(128)}, f32[4,8,256]{2,1,0:T(8,128)S(1)}, f32[4,8,256]{2,1,0:T(8,128)S(1)}, f32[4,8,256]{2,1,0:T(8,128)}, /*inde...) fusion(f32[10,14,262]{2,1,0:T(8,128)S(1)} %and_convert_fusion, ...), kind=kLoop, calls=%fused_computation.1996 | loop fusion | flops 9715710 | bytes 10428424 | tf_op jit(solution)/shard_map/reduce_sum | solution.py:235
  94.0 2.1 collective-permute-done.12
  97.3 3.8 %collective-permute-start.15 = (f32[2,10,3,256]{3,2,1,0:T(4,128)S(1)}, f32[2,10,3,256]{3,2,1,0:T(4,128)S(1)}, u32[]{:S(2)}, u32[]{:S(2)}) collective-permute-start(f32[2,10,3,256]{3,2,1,0:T(4,128)S(1)} %get-tuple-element.822), channel_id=1, source_target_pairs={{0,12},{1,13},{2,14},{3,15},{4,0},{5,1},{6,2},{7,3},{8,4},{9,5},{1... | collective-permute-start | bytes 184328 | tf_op jit(solution)/shard_map/ppermute | solution.py:26
  101.1 2.4 %collective-permute-done.14 = f32[2,10,3,256]{3,2,1,0:T(4,128)S(1)} collective-permute-done((f32[2,10,3,256]{3,2,1,0:T(4,128)S(1)}, f32[2,10,3,256]{3,2,1,0:T(4,128)S(1)}, u32[]{:S(2)}, u32[]{:S(2)}) %collective-permute-start.14) | collective-permute-done | bytes 61472 | tf_op jit(solution)/shard_map/ppermute | solution.py:26
  105.0 41.0 %all-reduce = (f32[]{:T(128)}, f32[]{:T(128)}) all-reduce(f32[]{:T(128)} %get-tuple-element.4, f32[]{:T(128)} %get-tuple-element.3), channel_id=1, replica_groups=mesh['gx'=2,'yz'=16] {'gx','yz'}, use_global_device_ids=true, to_apply=%region_1.2 | all-reduce | flops 2 | bytes 16 | tf_op jit(solution)/shard_map/psum | solution.py:234
  147.4 2.3 %collective-permute-start.17 = (f32[2,10,14,3]{3,2,1,0:T(8,128)}, f32[2,10,14,3]{3,2,1,0:T(8,128)S(1)}, u32[]{:S(2)}, u32[]{:S(2)}) collective-permute-start(f32[2,10,14,3]{3,2,1,0:T(8,128)} %get-tuple-element.813), channel_id=1, source_target_pairs={{0,15},{1,0},{2,1},{3,2},{4,3},{5,4},{6,5},{7,6},{8,7},{9,8},{10,9... | collective-permute-start | bytes 10088 | tf_op jit(solution)/shard_map/ppermute | solution.py:26
  150.7 2.2 %collective-permute-done.17 = f32[2,10,14,3]{3,2,1,0:T(8,128)S(1)} collective-permute-done((f32[2,10,14,3]{3,2,1,0:T(8,128)}, f32[2,10,14,3]{3,2,1,0:T(8,128)S(1)}, u32[]{:S(2)}, u32[]{:S(2)}) %collective-permute-start.17) | collective-permute-done | bytes 3392 | tf_op jit(solution)/shard_map/ppermute | solution.py:26
  176.2 5.7 %add_bitcast_fusion.3 = f32[1,4,8,256]{3,2,1,0:T(8,128)S(1)} fusion(f32[4,8,256]{2,1,0:T(8,128)S(1)} %get-tuple-element.843, f32[10,14,262]{2,1,0:T(8,128)S(1)} %get-tuple-element.806, f32[4,8,256]{2,1,0:T(8,128)} %get-tuple-element.816, f32[4,8,256]{2,1,0:T(8,128)S(1)} %copy-done.32, f32[4,8,256]{2,1,0:T(8,128)} %get-tuple-element.677, ...), kind=kLoop, calls=%fused_computation.1343 | loop fusion | flops 7995392 | bytes 8060928 | tf_op jit(solution)/shard_map/broadcast_in_dim | solution.py:202
  186.9 3.8 %collective-permute-start.21 = (f32[1,6,1,256]{3,2,1,0:T(1,128)S(1)}, f32[1,6,1,256]{3,2,1,0:T(1,128)S(1)}, u32[]{:S(2)}, u32[]{:S(2)}) collective-permute-start(f32[1,6,1,256]{3,2,1,0:T(1,128)S(1)} %get-tuple-element.840), channel_id=1, source_target_pairs={{0,12},{1,13},{2,14},{3,15},{4,0},{5,1},{6,2},{7,3},{8,4},{9,5},{1... | collective-permute-start | bytes 18440 | tf_op jit(solution)/shard_map/ppermute | solution.py:26
  192.6 4.7 %collective-permute-start.23 = (f32[1,6,10,1]{3,2,1,0:T(8,128)S(1)}, f32[1,6,10,1]{3,2,1,0:T(8,128)S(1)}, u32[]{:S(2)}, u32[]{:S(2)}) collective-permute-start(f32[1,6,10,1]{3,2,1,0:T(8,128)S(1)} %get-tuple-element.826), channel_id=1, source_target_pairs={{0,15},{1,0},{2,1},{3,2},{4,3},{5,4},{6,5},{7,6},{8,7},{9,8},{10,9... | collective-permute-start | bytes 728 | tf_op jit(solution)/shard_map/ppermute | solution.py:26
  202.0 3.3 %add_bitcast_fusion.1 = f32[1,4,1,8,256]{4,3,2,1,0:T(8,128)S(1)} fusion(f32[4,8,256]{2,1,0:T(8,128)S(1)} %get-tuple-element.417, f32[4,8,256]{2,1,0:T(8,128)S(1)} %copy-done.130, f32[4,8,256]{2,1,0:T(8,128)S(1)} %get-tuple-element.419, f32[4,8,256]{2,1,0:T(8,128)} %get-tuple-element.477, f32[4,8,256]{2,1,0:T(8,128)S(1)} %get-tuple-element.421, ...), kind=kLoop, calls=%fused_computation.1340 | loop fusion | flops 2228224 | bytes 8388608 | tf_op jit(solution)/shard_map/stack | solution.py:232
  206.4 3.5 %add_bitcast_fusion.2 = f32[1,4,1,8,256]{4,3,2,1,0:T(8,128)S(1)} fusion(f32[4,8,256]{2,1,0:T(8,128)S(1)} %get-tuple-element.417, f32[4,8,256]{2,1,0:T(8,128)S(1)} %copy-done.118, f32[4,8,256]{2,1,0:T(8,128)S(1)} %get-tuple-element.419, f32[4,8,256]{2,1,0:T(8,128)S(1)} %copy-done.109, f32[4,8,256]{2,1,0:T(8,128)S(1)} %get-tuple-element.421, ...), kind=kLoop, calls=%fused_computation.1342 | loop fusion | flops 2228224 | bytes 8388608 | tf_op jit(solution)/shard_map/stack | solution.py:232
  210.7 3.2 %add_bitcast_fusion = f32[1,4,1,8,256]{4,3,2,1,0:T(8,128)S(1)} fusion(f32[4,8,256]{2,1,0:T(8,128)S(1)} %get-tuple-element.417, f32[4,8,256]{2,1,0:T(8,128)} %get-tuple-element.673, f32[4,8,256]{2,1,0:T(8,128)S(1)} %get-tuple-element.419, f32[4,8,256]{2,1,0:T(8,128)S(1)} %get-tuple-element.364, f32[4,8,256]{2,1,0:T(8,128)S(1)} %get-tuple-element.421, ...), kind=kLoop, calls=%fused_computation.1338 | loop fusion | flops 2228224 | bytes 8388608 | tf_op jit(solution)/shard_map/stack | solution.py:232
  (484 shorter events, 91.4 us)
Async XLA Ops:
  1.6 5.5 %collective-permute-start = (f32[3,3,8,256]{3,2,1,0:T(8,128)S(1)}, f32[3,3,8,256]{3,2,1,0:T(8,128)S(1)}, u32[]{:S(2)}, u32[]{:S(2)}) collective-permute-start(f32[3,3,8,256]{3,2,1,0:T(8,128)S(1)} %get-tuple-element.833), channel_id=1, source_target_pairs={{0,16},{16,0},{1,17},{17,1},{2,18},{18,2},{3,19},{19,3},{4,20},{20... | collective-permute-start | bytes 221192 | tf_op jit(solution)/shard_map/ppermute | solution.py:26
  4.6 4.4 %collective-permute-start.1 = (f32[3,3,8,256]{3,2,1,0:T(8,128)S(1)}, f32[3,3,8,256]{3,2,1,0:T(8,128)S(1)}, u32[]{:S(2)}, u32[]{:S(2)}) collective-permute-start(f32[3,3,8,256]{3,2,1,0:T(8,128)S(1)} %get-tuple-element.834), channel_id=1, source_target_pairs={{0,16},{16,0},{1,17},{17,1},{2,18},{18,2},{3,19},{19,3},{4,20},{20... | collective-permute-start | bytes 221192 | tf_op jit(solution)/shard_map/ppermute | solution.py:26
  9.1 8.0 %collective-permute-start.2 = (f32[3,10,3,256]{3,2,1,0:T(4,128)S(1)}, f32[3,10,3,256]{3,2,1,0:T(4,128)S(1)}, u32[]{:S(2)}, u32[]{:S(2)}) collective-permute-start(f32[3,10,3,256]{3,2,1,0:T(4,128)S(1)} %get-tuple-element.819), channel_id=1, source_target_pairs={{0,4},{1,5},{2,6},{3,7},{4,8},{5,9},{6,10},{7,11},{8,12},{9,13},{1... | collective-permute-start | bytes 276488 | tf_op jit(solution)/shard_map/ppermute | solution.py:26
  10.8 7.0 %collective-permute-start.3 = (f32[3,10,3,256]{3,2,1,0:T(4,128)S(1)}, f32[3,10,3,256]{3,2,1,0:T(4,128)S(1)}, u32[]{:S(2)}, u32[]{:S(2)}) collective-permute-start(f32[3,10,3,256]{3,2,1,0:T(4,128)S(1)} %get-tuple-element.820), channel_id=1, source_target_pairs={{0,12},{1,13},{2,14},{3,15},{4,0},{5,1},{6,2},{7,3},{8,4},{9,5},{1... | collective-permute-start | bytes 276488 | tf_op jit(solution)/shard_map/ppermute | solution.py:26
  23.3 5.8 %collective-permute-start.4 = (f32[3,10,14,3]{3,2,1,0:T(8,128)S(1)}, f32[3,10,14,3]{3,2,1,0:T(8,128)S(1)}, u32[]{:S(2)}, u32[]{:S(2)}) collective-permute-start(f32[3,10,14,3]{3,2,1,0:T(8,128)S(1)} %get-tuple-element.810), channel_id=1, source_target_pairs={{0,15},{1,0},{2,1},{3,2},{4,3},{5,4},{6,5},{7,6},{8,7},{9,8},{10,9... | collective-permute-start | bytes 15128 | tf_op jit(solution)/shard_map/ppermute | solution.py:26
  26.1 8.3 %collective-permute-start.5 = (f32[3,10,14,3]{3,2,1,0:T(8,128)S(1)}, f32[3,10,14,3]{3,2,1,0:T(8,128)S(1)}, u32[]{:S(2)}, u32[]{:S(2)}) collective-permute-start(f32[3,10,14,3]{3,2,1,0:T(8,128)S(1)} %get-tuple-element.811), channel_id=1, source_target_pairs={{0,1},{1,2},{2,3},{3,4},{4,5},{5,6},{6,7},{7,8},{8,9},{9,10},{10,1... | collective-permute-start | bytes 15128 | tf_op jit(solution)/shard_map/ppermute | solution.py:26
  63.2 4.2 %collective-permute-start.6 = (f32[2,3,8,256]{3,2,1,0:T(8,128)S(1)}, f32[2,3,8,256]{3,2,1,0:T(8,128)S(1)}, u32[]{:S(2)}, u32[]{:S(2)}) collective-permute-start(f32[2,3,8,256]{3,2,1,0:T(8,128)S(1)} %get-tuple-element.837), channel_id=1, source_target_pairs={{0,16},{16,0},{1,17},{17,1},{2,18},{18,2},{3,19},{19,3},{4,20},{20... | collective-permute-start | bytes 147464 | tf_op jit(solution)/shard_map/ppermute | solution.py:26
  64.1 4.1 %collective-permute-start.7 = (f32[2,3,8,256]{3,2,1,0:T(8,128)S(1)}, f32[2,3,8,256]{3,2,1,0:T(8,128)S(1)}, u32[]{:S(2)}, u32[]{:S(2)}) collective-permute-start(f32[2,3,8,256]{3,2,1,0:T(8,128)S(1)} %get-tuple-element.838), channel_id=1, source_target_pairs={{0,16},{16,0},{1,17},{17,1},{2,18},{18,2},{3,19},{19,3},{4,20},{20... | collective-permute-start | bytes 147464 | tf_op jit(solution)/shard_map/ppermute | solution.py:26
  68.2 6.3 %collective-permute-start.8 = (f32[2,10,3,256]{3,2,1,0:T(4,128)S(1)}, f32[2,10,3,256]{3,2,1,0:T(4,128)S(1)}, u32[]{:S(2)}, u32[]{:S(2)}) collective-permute-start(f32[2,10,3,256]{3,2,1,0:T(4,128)S(1)} %get-tuple-element.823), channel_id=1, source_target_pairs={{0,4},{1,5},{2,6},{3,7},{4,8},{5,9},{6,10},{7,11},{8,12},{9,13},{1... | collective-permute-start | bytes 184328 | tf_op jit(solution)/shard_map/ppermute | solution.py:26
  68.3 6.2 %collective-permute-start.9 = (f32[2,10,3,256]{3,2,1,0:T(4,128)S(1)}, f32[2,10,3,256]{3,2,1,0:T(4,128)S(1)}, u32[]{:S(2)}, u32[]{:S(2)}) collective-permute-start(f32[2,10,3,256]{3,2,1,0:T(4,128)S(1)} %get-tuple-element.824), channel_id=1, source_target_pairs={{0,12},{1,13},{2,14},{3,15},{4,0},{5,1},{6,2},{7,3},{8,4},{9,5},{1... | collective-permute-start | bytes 184328 | tf_op jit(solution)/shard_map/ppermute | solution.py:26
  74.7 7.5 %collective-permute-start.10 = (f32[2,10,14,3]{3,2,1,0:T(8,128)S(1)}, f32[2,10,14,3]{3,2,1,0:T(8,128)S(1)}, u32[]{:S(2)}, u32[]{:S(2)}) collective-permute-start(f32[2,10,14,3]{3,2,1,0:T(8,128)S(1)} %get-tuple-element.814), channel_id=1, source_target_pairs={{0,1},{1,2},{2,3},{3,4},{4,5},{5,6},{6,7},{7,8},{8,9},{9,10},{10,1... | collective-permute-start | bytes 10088 | tf_op jit(solution)/shard_map/ppermute | solution.py:26
  75.6 7.3 %collective-permute-start.11 = (f32[2,10,14,3]{3,2,1,0:T(8,128)S(1)}, f32[2,10,14,3]{3,2,1,0:T(8,128)S(1)}, u32[]{:S(2)}, u32[]{:S(2)}) collective-permute-start(f32[2,10,14,3]{3,2,1,0:T(8,128)S(1)} %get-tuple-element.815), channel_id=1, source_target_pairs={{0,15},{1,0},{2,1},{3,2},{4,3},{5,4},{6,5},{7,6},{8,7},{9,8},{10,9... | collective-permute-start | bytes 10088 | tf_op jit(solution)/shard_map/ppermute | solution.py:26
  91.9 4.2 %collective-permute-start.12 = (f32[2,3,8,256]{3,2,1,0:T(8,128)S(1)}, f32[2,3,8,256]{3,2,1,0:T(8,128)S(1)}, u32[]{:S(2)}, u32[]{:S(2)}) collective-permute-start(f32[2,3,8,256]{3,2,1,0:T(8,128)S(1)} %get-tuple-element.835), channel_id=1, source_target_pairs={{0,16},{16,0},{1,17},{17,1},{2,18},{18,2},{3,19},{19,3},{4,20},{20... | collective-permute-start | bytes 147464 | tf_op jit(solution)/shard_map/ppermute | solution.py:26
  93.1 4.1 %collective-permute-start.13 = (f32[2,3,8,256]{3,2,1,0:T(8,128)S(1)}, f32[2,3,8,256]{3,2,1,0:T(8,128)S(1)}, u32[]{:S(2)}, u32[]{:S(2)}) collective-permute-start(f32[2,3,8,256]{3,2,1,0:T(8,128)S(1)} %get-tuple-element.836), channel_id=1, source_target_pairs={{0,16},{16,0},{1,17},{17,1},{2,18},{18,2},{3,19},{19,3},{4,20},{20... | collective-permute-start | bytes 147464 | tf_op jit(solution)/shard_map/ppermute | solution.py:26
  97.3 6.3 %collective-permute-start.14 = (f32[2,10,3,256]{3,2,1,0:T(4,128)S(1)}, f32[2,10,3,256]{3,2,1,0:T(4,128)S(1)}, u32[]{:S(2)}, u32[]{:S(2)}) collective-permute-start(f32[2,10,3,256]{3,2,1,0:T(4,128)S(1)} %get-tuple-element.821), channel_id=1, source_target_pairs={{0,4},{1,5},{2,6},{3,7},{4,8},{5,9},{6,10},{7,11},{8,12},{9,13},{1... | collective-permute-start | bytes 184328 | tf_op jit(solution)/shard_map/ppermute | solution.py:26
  97.3 6.2 %collective-permute-start.15 = (f32[2,10,3,256]{3,2,1,0:T(4,128)S(1)}, f32[2,10,3,256]{3,2,1,0:T(4,128)S(1)}, u32[]{:S(2)}, u32[]{:S(2)}) collective-permute-start(f32[2,10,3,256]{3,2,1,0:T(4,128)S(1)} %get-tuple-element.822), channel_id=1, source_target_pairs={{0,12},{1,13},{2,14},{3,15},{4,0},{5,1},{6,2},{7,3},{8,4},{9,5},{1... | collective-permute-start | bytes 184328 | tf_op jit(solution)/shard_map/ppermute | solution.py:26
  105.0 44.7 %collective-permute-start.16 = (f32[2,10,14,3]{3,2,1,0:T(8,128)}, f32[2,10,14,3]{3,2,1,0:T(8,128)}, u32[]{:S(2)}, u32[]{:S(2)}) collective-permute-start(f32[2,10,14,3]{3,2,1,0:T(8,128)} %get-tuple-element.812), channel_id=1, source_target_pairs={{0,1},{1,2},{2,3},{3,4},{4,5},{5,6},{6,7},{7,8},{8,9},{9,10},{10,1... | collective-permute-start | bytes 10088 | tf_op jit(solution)/shard_map/ppermute | solution.py:26
  147.4 5.5 %collective-permute-start.17 = (f32[2,10,14,3]{3,2,1,0:T(8,128)}, f32[2,10,14,3]{3,2,1,0:T(8,128)S(1)}, u32[]{:S(2)}, u32[]{:S(2)}) collective-permute-start(f32[2,10,14,3]{3,2,1,0:T(8,128)} %get-tuple-element.813), channel_id=1, source_target_pairs={{0,15},{1,0},{2,1},{3,2},{4,3},{5,4},{6,5},{7,6},{8,7},{9,8},{10,9... | collective-permute-start | bytes 10088 | tf_op jit(solution)/shard_map/ppermute | solution.py:26
  181.9 4.0 %collective-permute-start.18 = (f32[1,1,8,256]{3,2,1,0:T(8,128)S(1)}, f32[1,1,8,256]{3,2,1,0:T(8,128)S(1)}, u32[]{:S(2)}, u32[]{:S(2)}) collective-permute-start(f32[1,1,8,256]{3,2,1,0:T(8,128)S(1)} %get-tuple-element.841), channel_id=1, source_target_pairs={{0,16},{16,0},{1,17},{17,1},{2,18},{18,2},{3,19},{19,3},{4,20},{20... | collective-permute-start | bytes 24584 | tf_op jit(solution)/shard_map/ppermute | solution.py:26
  183.2 3.7 %collective-permute-start.19 = (f32[1,1,8,256]{3,2,1,0:T(8,128)S(1)}, f32[1,1,8,256]{3,2,1,0:T(8,128)S(1)}, u32[]{:S(2)}, u32[]{:S(2)}) collective-permute-start(f32[1,1,8,256]{3,2,1,0:T(8,128)S(1)} %get-tuple-element.842), channel_id=1, source_target_pairs={{0,16},{16,0},{1,17},{17,1},{2,18},{18,2},{3,19},{19,3},{4,20},{20... | collective-permute-start | bytes 24584 | tf_op jit(solution)/shard_map/ppermute | solution.py:26
  186.8 5.5 %collective-permute-start.20 = (f32[1,6,1,256]{3,2,1,0:T(1,128)S(1)}, f32[1,6,1,256]{3,2,1,0:T(1,128)S(1)}, u32[]{:S(2)}, u32[]{:S(2)}) collective-permute-start(f32[1,6,1,256]{3,2,1,0:T(1,128)S(1)} %get-tuple-element.839), channel_id=1, source_target_pairs={{0,4},{1,5},{2,6},{3,7},{4,8},{5,9},{6,10},{7,11},{8,12},{9,13},{1... | collective-permute-start | bytes 18440 | tf_op jit(solution)/shard_map/ppermute | solution.py:26
  186.9 5.4 %collective-permute-start.21 = (f32[1,6,1,256]{3,2,1,0:T(1,128)S(1)}, f32[1,6,1,256]{3,2,1,0:T(1,128)S(1)}, u32[]{:S(2)}, u32[]{:S(2)}) collective-permute-start(f32[1,6,1,256]{3,2,1,0:T(1,128)S(1)} %get-tuple-element.840), channel_id=1, source_target_pairs={{0,12},{1,13},{2,14},{3,15},{4,0},{5,1},{6,2},{7,3},{8,4},{9,5},{1... | collective-permute-start | bytes 18440 | tf_op jit(solution)/shard_map/ppermute | solution.py:26
  192.4 6.2 %collective-permute-start.22 = (f32[1,6,10,1]{3,2,1,0:T(8,128)S(1)}, f32[1,6,10,1]{3,2,1,0:T(8,128)S(1)}, u32[]{:S(2)}, u32[]{:S(2)}) collective-permute-start(f32[1,6,10,1]{3,2,1,0:T(8,128)S(1)} %get-tuple-element.825), channel_id=1, source_target_pairs={{0,1},{1,2},{2,3},{3,4},{4,5},{5,6},{6,7},{7,8},{8,9},{9,10},{10,1... | collective-permute-start | bytes 728 | tf_op jit(solution)/shard_map/ppermute | solution.py:26
  192.6 6.5 %collective-permute-start.23 = (f32[1,6,10,1]{3,2,1,0:T(8,128)S(1)}, f32[1,6,10,1]{3,2,1,0:T(8,128)S(1)}, u32[]{:S(2)}, u32[]{:S(2)}) collective-permute-start(f32[1,6,10,1]{3,2,1,0:T(8,128)S(1)} %get-tuple-element.826), channel_id=1, source_target_pairs={{0,15},{1,0},{2,1},{3,2},{4,3},{5,4},{6,5},{7,6},{8,7},{9,8},{10,9... | collective-permute-start | bytes 728 | tf_op jit(solution)/shard_map/ppermute | solution.py:26
  (166 other events, 1721.4 us)
where the time goes:
time: 219 us; the launch traced here: 216 us
  other arithmetic  88.9 us (41%)
  blocking collectives  41 us (19%)
  starting transfers between devices  38.5 us (18%)
  waiting for transfers between devices  34.1 us (16%)
  local copies, waits for them, and re-layouts  7.64 us (3%)
  between operations  5.58 us (3%)
    psum x1, blocking collectives, body(): lax.psum((jnp.sum(own_present * jnp.exp(bias_energy / THERMAL)), jnp.sum(...  41 us
    ppermute x24, starting transfers between devices, from_behind(): return lax.ppermute(x, axis, [(i, (i + by) % size) for i in range(size)])  38.5 us
    ppermute x24, waiting for transfers between devices, from_behind(): return lax.ppermute(x, axis, [(i, (i + by) % size) for i in range(size)])  34.1 us
    sqrt x41, other arithmetic, separation(): jnp.sqrt(pieces[0] * pieces[0] + pieces[1] * pieces[1] + pieces[2] * piec...  34.1 us
    div x24, other arithmetic, reach_forces(): (adjoint_total * far_energy + far_adjoint * bond_energy) * taper_slope(ra...  22.2 us
    another operation x3, other arithmetic, body(): half_velocity = own_velocity + KICK_FACTOR * jnp.stack(forces)  10.1 us
    reduce_sum x1, other arithmetic, body(): jnp.sum(own_present)  7.43 us
    broadcast_in_dim x1, other arithmetic, body(): padded_lambda = add_ghosts(adjoint_lambda[None], 1, z_tile)[0]  5.73 us
  transfers between devices with their start and end apart: 24, of which 19 were waited for; matrix products, arithmetic and copies ran while one was open for 3% of the time, Pallas kernels for 0%

commit v1 on v0

v1 whole, which is shorter than its diff:
```python
import functools

import jax
import jax.numpy as jnp
from jax import lax
from jax.experimental import pallas as pl
from jax.experimental.pallas import tpu as pltpu
from jax.sharding import PartitionSpec as P

CUTOFF_SQ = 1.5 * 1.5
REACH_SQ = 3.5 * 3.5
F32 = jnp.float32
MESH = pl.DeviceIdType.MESH


def list_offsets(reach_sq, forward_only):
    chosen = []
    for ax in range(-3, 4):
        for ay in range(-3, 4):
            for az in range(-3, 4):
                length_sq = ax * ax + ay * ay + az * az
                if 0 < length_sq <= reach_sq:
                    if not forward_only or (ax, ay, az) > (0, 0, 0):
                        chosen.append((ax, ay, az))
    return chosen


FORWARD = list_offsets(2, True)
BONDS = FORWARD + [(-v[0], -v[1], -v[2]) for v in FORWARD]
REACH = list_offsets(9, False)
ROUNDS = [(3, 0, 3), (1, 3, 3), (1, 4, 3), (1, 5, 1), (2, 6, 1)]


def kernel(n_gx, n_yz, z_tiles, heights, disp, vel, rest, new_disp, new_vel, boost, *scratch):
    xr, yr, zr, ys, zs = (scratch[i:25:5] for i in range(5))
    (store, zb, hb, ins, bonds, part, first, sums, send_sem, recv_sem, red_send, red_recv) = scratch[25:]
    nx_all, ny_all = heights.shape
    planes, rows, cols = disp.shape[1], disp.shape[3], disp.shape[4]
    y_tiles = n_yz // z_tiles
    gx = lax.axis_index("gx")
    me = lax.axis_index("yz")
    h = me + z_tiles // 2
    y_tile = lax.rem(h // z_tiles, y_tiles)
    z_tile = lax.rem(h, z_tiles)
    x_steps = [0, 1] if n_gx == 2 else [0, 1, -1]
    n_slots = len(x_steps)
    steps = [0, 1, -1]

    def target(a, b, c):
        to_y = lax.rem(y_tile + b + y_tiles, y_tiles)
        to_z = lax.rem(z_tile + c + z_tiles, z_tiles)
        to = lax.rem(to_y * z_tiles + to_z + n_yz - z_tiles // 2, n_yz)
        return (lax.rem(gx + a + n_gx, n_gx), to)

    n_dev = n_gx * n_yz
    rank = gx * n_yz + me
    barrier = pltpu.get_barrier_semaphore()

    def greet(k, carry):
        to = lax.rem(rank + k, n_dev)
        pl.semaphore_signal(barrier, inc=1, device_id=(to // n_yz, lax.rem(to, n_yz)), device_id_type=MESH)
        return carry

    lax.fori_loop(1, n_dev, greet, 0)

    lane = lax.broadcasted_iota(jnp.int32, (8, 128), 1)

    def messages(r):
        out = []
        for ai, a in enumerate(x_steps):
            if ai:
                out.append((xr[r].at[0], xr[r].at[ai], a, 0, 0))
        for bi in range(2):
            for ai, a in enumerate(x_steps):
                out.append((ys[r].at[bi], yr[r].at[bi, ai], a, steps[1 + bi], 0))
        for ci in range(2):
            for bi, b in enumerate(steps):
                for ai, a in enumerate(x_steps):
                    out.append((zs[r].at[ci], zr[r].at[ci, bi, ai], a, b, steps[1 + ci]))
        return [
            pltpu.make_async_remote_copy(
                src_ref=src,
                dst_ref=dst,
                send_sem=send_sem.at[r, i],
                recv_sem=recv_sem.at[r, i],
                device_id=target(a, b, c),
                device_id_type=MESH,
            )
            for i, (src, dst, a, b, c) in enumerate(out)
        ]

    def pack(r):
        count = ROUNDS[r][0]
        up = jnp.zeros((8, 128), F32)
        down = jnp.zeros((8, 128), F32)
        for q in range(count):
            for p in range(planes):
                item = q * planes + p
                low = xr[r][0, q, p, :, 0:128]
                high = xr[r][0, q, p, :, cols - 128 : cols]
                here = (lane >= 4 * item) & (lane < 4 * item + 4)
                up = jnp.where(here, pltpu.roll(high, (4 * item + 4) % 128, 1), up)
                down = jnp.where(here, pltpu.roll(low, (4 * item) % 128, 1), down)
                ys[r][0, q, p] = xr[r][0, q, p, rows - 4 : rows, :]
                ys[r][1, q, p] = xr[r][0, q, p, 0:4, :]
        zs[r][0] = up
        zs[r][1] = down

    def send(r):
        pack(r)
        for copy in messages(r):
            copy.start()

    def receive(r):
        for copy in messages(r):
            copy.wait_recv()
        count, base, halo = ROUNDS[r]
        for ai in range(n_slots):
            for ci in range(2):
                inside = z_tile > 0 if ci == 0 else z_tile < z_tiles - 1
                keep = jnp.where(inside, 1.0, 0.0).astype(F32)
                zb[ai, ci, 4:12] = zr[r][ci, 0, ai] * keep
                zb[ai, ci, 0:4] = zr[r][ci, 1, ai, 4:8] * keep
                zb[ai, ci, 12:16] = zr[r][ci, 2, ai, 0:4] * keep

        def one(xp, carry):
            plane = lax.rem(xp + 1, planes)
            group = (xp + 1) // planes
            slot = lax.rem(group + 1, 2) if n_gx == 2 else lax.rem(4 - group, 3)
            for q in range(count):
                for half in range(2):
                    span = slice(half * 128, half * 128 + 128)
                    store[base + q, 3, half, xp, 4:12] = xr[r][slot, q, plane, :, span]
                    store[base + q, 3, half, xp, 0:4] = yr[r][0, slot, q, plane, :, span]
                    store[base + q, 3, half, xp, 12:16] = yr[r][1, slot, q, plane, :, span]
            for q in range(count):
                item = q * planes + plane
                for rt in range(2):
                    band = slice(8 * rt, 8 * rt + 8)
                    t1 = store[base + q, 3, 0, xp, band]
                    t2 = store[base + q, 3, 1, xp, band]
                    below = zb[slot, 0, band]
                    above = zb[slot, 1, band]
                    for dz in range(1, halo + 1):
                        r0 = pltpu.roll(below, lax.rem(124 + 128 - 4 * item + dz, 128), 1)
                        r1 = pltpu.roll(t1, dz, 1)
                        r2 = pltpu.roll(t2, dz, 1)
                        store[base + q, 3 - dz, 0, xp, band] = jnp.where(lane < dz, r0, r1)
                        store[base + q, 3 - dz, 1, xp, band] = jnp.where(lane < dz, r1, r2)
                        s1 = pltpu.roll(t1, 128 - dz, 1)
                        s2 = pltpu.roll(t2, 128 - dz, 1)
                        s3 = pltpu.roll(above, lax.rem(256 - 4 * item - dz, 128), 1)
                        store[base + q, 3 + dz, 0, xp, band] = jnp.where(lane >= 128 - dz, s2, s1)
                        store[base + q, 3 + dz, 1, xp, band] = jnp.where(lane >= 128 - dz, s3, s2)
            return carry

        lax.fori_loop(3 - halo, 3 + planes + halo, one, 0)

    def far(q, x, half, d):
        return store[q, d[2] + 3, half, x + 3 + d[0], 4 + d[1] : 12 + d[1]]

    def separation(x, half, d, mine):
        pieces = []
        for c in range(3):
            delta = far(c, x, half, d) - mine[c]
            pieces.append(delta + float(d[c]) if d[c] else delta)
        return pieces

    def own(q, x, half):
        return far(q, x, half, (0, 0, 0))

    def put(ref, q, x, half, value):
        @pl.when(half == 0)
        def _():
            ref[0, q, x, :, 0:128] = value

        @pl.when(half == 1)
        def _():
            ref[0, q, x, :, 128:256] = value

    def tiles(body):
        def step(i, carry):
            body(i, i // 2, lax.rem(i, 2))
            return carry

        lax.fori_loop(0, 2 * planes, step, 0)

    for q in range(3):
        for p in range(planes):
            xr[0][0, q, p] = disp[q, p, 0]

    def height_row(xp, carry):
        at_x = lax.rem(gx * planes + xp - 3 + nx_all, nx_all)
        for row in range(3, 13):
            at_y = lax.rem(y_tile * rows + row - 4 + ny_all, ny_all)
            hb[xp, row : row + 1] = jnp.full((1, 128), heights[at_x, at_y], jnp.int32)
        return carry

    lax.fori_loop(2, 4 + planes, height_row, 0)
    pl.semaphore_wait(barrier, n_dev - 1)
    send(0)
    receive(0)

    def bond_pass(i, x, half):
        mine = [own(c, x, half) for c in range(3)]
        layer = lane + (z_tile * cols + half * 128)
        here = layer < hb[x + 3, 4:12]
        density = jnp.zeros((8, 128), F32)
        energy = jnp.zeros((8, 128), F32)
        room = jnp.zeros((8, 128), F32)
        for k, d in enumerate(BONDS):
            s = separation(x, half, d, mine)
            r_sq = s[0] * s[0] + s[1] * s[1] + s[2] * s[2]
            inv_r = lax.rsqrt(r_sq)
            radius = r_sq * inv_r
            partner = layer + d[2] < hb[x + 3 + d[0], 4 + d[1] : 12 + d[1]]
            if d[2] < 0:
                partner = partner & (layer >= -d[2])
            paired = partner & here
            decay = jnp.exp(3.0 - 3.0 * radius)
            cut = jnp.maximum(1.0 - r_sq * (1.0 / CUTOFF_SQ), 0.0)
            cut_value = cut * cut
            length = rest_half(k, x, half)
            gain = 10.0 / length
            strain = (radius - length) * gain
            squared = strain * strain
            lifted = jnp.exp(8.0 * squared)
            density = density + jnp.where(partner, decay * cut_value, 0.0)
            energy = energy + jnp.where(paired, lifted, 0.0)
            room = room + jnp.where(paired, 1.0 - squared, 0.0)
            scale = jnp.where(paired, inv_r, 0.0)
            cut_slope = (-4.0 / CUTOFF_SQ) * radius * cut
            bonds[i, k, 0] = scale * 0.6 * (decay * decay) * (cut_slope - 6.0 * cut_value)
            bonds[i, k, 1] = scale * decay * (cut_slope - 3.0 * cut_value)
            strain_slope = scale * (2.0 * strain * gain)
            bonds[i, k, 2] = strain_slope * (8.0 * lifted)
            bonds[i, k, 3] = strain_slope
        put(xr[1], 0, x, half, energy)
        put(xr[4], 0, x, half, -0.5 * lax.rsqrt(density + 0.5))
        part[i, 0] = room

    def rest_half(k, x, half):
        return rest[k, x, 0, :, pl.ds(pl.multiple_of(half * 128, 128), 128)]

    tiles(bond_pass)
    send(1)

    def reach_pass(i, x, half):
        mine = [own(c, x, half) for c in range(3)]
        for k, d in enumerate(REACH):
            s = separation(x, half, d, mine)
            r_sq = s[0] * s[0] + s[1] * s[1] + s[2] * s[2]
            ins[i, k] = jnp.maximum(1.0 - r_sq * (1.0 / REACH_SQ), 0.0)

    tiles(reach_pass)
    receive(1)
    first[...] = jnp.zeros_like(first)

    def smooth_pass(i, x, half):
        energy = own(3, x, half)
        total = 1.0 + energy
        for k, d in enumerate(REACH):
            inside = ins[i, k]
            total = total + (inside * inside) * far(3, x, half, d)
        room = part[i, 0]
        smooth = jnp.log(total) * 0.125
        share = 1.0 / (1.0 + smooth * smooth)
        gain = 0.08 * share
        layer = lane + (z_tile * cols + half * 128)
        here = layer < hb[x + 3, 4:12]
        adjoint = room * 0.08 * (-2.0 * smooth) * (share * share) / (8.0 * total)
        put(xr[2], 0, x, half, jnp.where(here, adjoint, 0.0))
        put(xr[4], 1, x, half, gain)
        first[...] += jnp.where(here, jnp.exp(gain * room * 2.0), 0.0)

    tiles(smooth_pass)
    send(2)
    send(4)
    sums[0] = jnp.sum(first[...], axis=0, keepdims=True)

    def reduction(k):
        to = lax.rem(rank + k, n_dev)
        return pltpu.make_async_remote_copy(
            src_ref=sums.at[0],
            dst_ref=sums.at[k],
            send_sem=red_send.at[k],
            recv_sem=red_recv.at[k],
            device_id=(to // n_yz, lax.rem(to, n_yz)),
            device_id_type=MESH,
        )

    def spread(k, carry):
        reduction(k).start()
        return carry

    lax.fori_loop(1, n_dev, spread, 0)

    def pull(source):
        def run(i, x, half):
            mine = [own(c, x, half) for c in range(3)]
            total = [jnp.zeros((8, 128), F32) for _ in range(3)]
            for k, d in enumerate(REACH):
                s = separation(x, half, d, mine)
                weight = ins[i, k] * far(source, x, half, d)
                total = [total[c] + weight * s[c] for c in range(3)]
            return total

        return run

    def energy_pull(i, x, half):
        total = pull(3)(i, x, half)
        for c in range(3):
            part[i, 1 + c] = total[c]

    tiles(energy_pull)
    receive(2)

    def lambda_pass(i, x, half):
        total = own(4, x, half)
        for k, d in enumerate(REACH):
            inside = ins[i, k]
            total = total + (inside * inside) * far(4, x, half, d)
        put(xr[3], 0, x, half, total)

    tiles(lambda_pass)
    send(3)

    def adjoint_pull(i, x, half):
        total = pull(4)(i, x, half)
        adjoint = own(4, x, half)
        energy = own(3, x, half)
        for c in range(3):
            part[i, 1 + c] = (-4.0 / REACH_SQ) * (adjoint * part[i, 1 + c] + energy * total[c])

    tiles(adjoint_pull)
    receive(4)
    receive(3)

    def final_pass(i, x, half):
        mine = [own(c, x, half) for c in range(3)]
        lam, embed, gain = own(5, x, half), own(6, x, half), own(7, x, half)
        force = [part[i, 1 + c] for c in range(3)]
        for k, d in enumerate(BONDS):
            s = separation(x, half, d, mine)
            weight = (
                bonds[i, k, 0]
                + (embed + far(6, x, half, d)) * bonds[i, k, 1]
                + (lam + far(5, x, half, d)) * bonds[i, k, 2]
                - (gain + far(7, x, half, d)) * bonds[i, k, 3]
            )
            force = [force[c] + weight * s[c] for c in range(3)]
        span = pl.ds(pl.multiple_of(half * 128, 128), 128)
        for c in range(3):
            speed = vel[c, x, 0, :, span] + 0.2 * force[c]
            new_vel[c, x, 0, :, span] = speed
            new_disp[c, x, 0, :, span] = mine[c] + 0.05 * speed

    tiles(final_pass)

    def collect(k, carry):
        reduction(k).wait_recv()
        return carry

    lax.fori_loop(1, n_dev, collect, 0)
    atoms = jnp.zeros((), jnp.int32)

    def count_row(i, carry):
        return carry + jnp.clip(heights[i // ny_all, lax.rem(i, ny_all)], 0, z_tiles * cols)

    atoms = lax.fori_loop(0, nx_all * ny_all, count_row, atoms)
    total = jnp.sum(jnp.sum(sums[...], axis=0), axis=1, keepdims=True)
    boost[...] = jnp.broadcast_to(total, (1, 128)) / jnp.full((1, 128), atoms.astype(F32))

    def finish(k, carry):
        reduction(k).wait_send()
        return carry

    lax.fori_loop(1, n_dev, finish, 0)
    for r in range(5):
        for copy in messages(r):
            copy.wait_send()


def body(n_gx, n_yz, displacement, velocity, rest_length, heights):
    _, planes, _, rows, cols = displacement.shape
    z_tiles = n_yz // (heights.shape[1] // rows)
    slots = 2 if n_gx == 2 else 3
    n_dev = n_gx * n_yz
    n_msg = (slots - 1) + 2 * slots + 6 * slots
    scratch = []
    for count, _, _ in ROUNDS:
        scratch += [
            pltpu.VMEM((slots, count, planes, rows, cols), F32),
            pltpu.VMEM((2, slots, count, planes, 4, cols), F32),
            pltpu.VMEM((2, 3, slots, 8, 128), F32),
            pltpu.VMEM((2, count, planes, 4, cols), F32),
            pltpu.VMEM((2, 8, 128), F32),
        ]
    scratch += [
        pltpu.VMEM((8, 7, 2, planes + 6, 16, 128), F32),
        pltpu.VMEM((slots, 2, 16, 128), F32),
        pltpu.VMEM((planes + 6, 16, 128), jnp.int32),
        pltpu.VMEM((2 * planes, len(REACH), 8, 128), F32),
        pltpu.VMEM((2 * planes, len(BONDS), 4, 8, 128), F32),
        pltpu.VMEM((2 * planes, 4, 8, 128), F32),
        pltpu.VMEM((8, 128), F32),
        pltpu.VMEM((n_dev, 1, 128), F32),
        pltpu.SemaphoreType.DMA((len(ROUNDS), n_msg)),
        pltpu.SemaphoreType.DMA((len(ROUNDS), n_msg)),
        pltpu.SemaphoreType.DMA((n_dev,)),
        pltpu.SemaphoreType.DMA((n_dev,)),
    ]
    vmem = pl.BlockSpec(memory_space=pltpu.VMEM)
    new_disp, new_vel, boost = pl.pallas_call(
        functools.partial(kernel, n_gx, n_yz, z_tiles),
        out_shape=(
            jax.ShapeDtypeStruct(displacement.shape, F32),
            jax.ShapeDtypeStruct(velocity.shape, F32),
            jax.ShapeDtypeStruct((1, 128), F32),
        ),
        in_specs=[pl.BlockSpec(memory_space=pltpu.SMEM), vmem, vmem, vmem],
        out_specs=(vmem, vmem, vmem),
        scratch_shapes=scratch,
        compiler_params=pltpu.CompilerParams(
            collective_id=0, has_side_effects=True, vmem_limit_bytes=48 * 1024 * 1024
        ),
    )(heights, displacement, velocity, rest_length)
    return new_disp, new_vel, boost[0, 0]


def solution(mesh):
    tiled = P(None, "gx", "yz", None, None)
    sizes = (mesh.shape["gx"], mesh.shape["yz"])
    return jax.shard_map(
        functools.partial(body, *sizes),
        mesh=mesh,
        in_specs=(tiled, tiled, tiled, P()),
        out_specs=(tiled, tiled, P()),
        check_vma=False,
    )
```

time: 219 us -> 55.6 us (0.25); the launches traced: 216 us -> 55.3 us
  other arithmetic: 88.9 us -> 0 us
  Pallas kernels: 0 us -> 48.7 us
  blocking collectives: 41 us -> 0 us
  starting transfers between devices: 38.5 us -> 0 us
  waiting for transfers between devices: 34.1 us -> 0 us
  between operations: 5.58 us -> 1.82 us
  local copies, waits for them, and re-layouts: 7.64 us -> 4.81 us
    pallas_call x0 -> x1, Pallas kernels: none -> 48.7 us  [body(): pl.pallas_call(functools.partial(kernel, n_gx, n_yz, z_tiles), out_shape=...]
    psum x1 -> x0, blocking collectives: 41 us -> none  [body(): lax.psum((jnp.sum(own_present * jnp.exp(bias_energy / THERMAL)), jnp.sum(...]
    ppermute x24 -> x0, starting transfers between devices: 38.5 us -> none  [from_behind(): return lax.ppermute(x, axis, [(i, (i + by) % size) for i in range(size)])]
    ppermute x24 -> x0, waiting for transfers between devices: 34.1 us -> none  [from_behind(): return lax.ppermute(x, axis, [(i, (i + by) % size) for i in range(size)])]
    sqrt x41 -> x0, other arithmetic: 34.1 us -> none  [separation(): jnp.sqrt(pieces[0] * pieces[0] + pieces[1] * pieces[1] + pieces[2] * piec...]
    div x35 -> x0, other arithmetic: 25.7 us -> none  [the longest x24 22.2 us: reach_forces(): (adjoint_total * far_energy + far_adjoint * bond_energy) * taper_slope(ra...]
    another operation x5 -> x0, other arithmetic: 10.1 us -> none  [the longest x3 10.1 us: body(): half_velocity = own_velocity + KICK_FACTOR * jnp.stack(forces)]
    reduce_sum x1 -> x0, other arithmetic: 7.43 us -> none  [body(): jnp.sum(own_present)]
  transfers between devices with their start and end apart: 24 -> 0, of which waited for: 19 -> 0; matrix products, arithmetic and copies ran while one was open for 3% -> 0% of each run, Pallas kernels for 0% -> 0%
where the time goes in v1:
time: 55.6 us; the launch traced here: 55.3 us
  Pallas kernels  48.7 us (88%)
  local copies, waits for them, and re-layouts  4.81 us (9%)
  between operations  1.82 us (3%)
    pallas_call x1, Pallas kernels, body(): pl.pallas_call(functools.partial(kernel, n_gx, n_yz, z_tiles), out_shape=...  48.7 us
    unnamed x10, local copies, waits for them, and re-layouts  4.81 us

profile of v1, /device:TPU:0, one launch (start us, length us, event | category | flops | bytes accessed | tf_op | source)
XLA Modules:
  0.0 55.3 jit_solution(4963986277320865669)
XLA Ops:
  0.6 0.0 copy-start
  0.6 1.1 %copy-done = f32[18,4,1,8,256]{4,3,2,1,0:T(8,128)S(1)} copy-done((f32[18,4,1,8,256]{4,3,2,1,0:T(8,128)S(1)}, f32[18,4,1,8,256]{4,3,2,1,0:T(8,128)}, u32[]{:S(2)}) %copy-start) | copy-done | bytes 589848
  1.7 0.0 copy-start.1
  1.7 0.9 %copy-done.1 = f32[3,4,1,8,256]{4,3,2,1,0:T(8,128)S(1)} copy-done((f32[3,4,1,8,256]{4,3,2,1,0:T(8,128)S(1)}, f32[3,4,1,8,256]{4,3,2,1,0:T(8,128)}, u32[]{:S(2)}) %copy-start.1) | copy-done | bytes 98328
  2.6 0.0 copy-start.2
  2.6 0.9 %copy-done.2 = f32[3,4,1,8,256]{4,3,2,1,0:T(8,128)S(1)} copy-done((f32[3,4,1,8,256]{4,3,2,1,0:T(8,128)S(1)}, f32[3,4,1,8,256]{4,3,2,1,0:T(8,128)}, u32[]{:S(2)}) %copy-start.2) | copy-done | bytes 98328
  3.5 0.0 copy-start.3
  3.5 0.7 %copy-done.3 = s32[8,32]{1,0:T(8,128)S(1)} copy-done((s32[8,32]{1,0:T(8,128)S(1)}, s32[8,32]{1,0:T(8,128)}, u32[]{:S(2)}) %copy-start.3) | copy-done | bytes 1048
  4.2 48.7 %shard_map.67 = (f32[3,4,1,8,256]{4,3,2,1,0:T(8,128)S(1)}, f32[3,4,1,8,256]{4,3,2,1,0:T(8,128)S(1)}, f32[1,128]{1,0:T(1,128)S(1)}) custom-call(s32[8,32]{1,0:T(8,128)S(1)} %copy-done.3, f32[3,4,1,8,256]{4,3,2,1,0:T(8,128)S(1)} %copy-done.1, f32[3,4,1,8,256]{4,3,2,1,0:T(8,128)S(1)} %copy-done.2, f32[18,4,1,8,256]{4,3,2,1,0:T(8,128)S(1)} %copy-done), custom_call_target="tpu_custom_call" | custom-call | tf_op jit(solution)/shard_map/pallas_call | solution.py:414
  52.9 0.6 %copy.10 = f32[3,4,1,8,256]{4,3,2,1,0:T(8,128)} copy(f32[3,4,1,8,256]{4,3,2,1,0:T(8,128)S(1)} %get-tuple-element.12) | data formatting | bytes 196608
  53.5 0.6 %copy.11 = f32[3,4,1,8,256]{4,3,2,1,0:T(8,128)} copy(f32[3,4,1,8,256]{4,3,2,1,0:T(8,128)S(1)} %get-tuple-element.13) | data formatting | bytes 196608
Async XLA Ops:
  0.6 1.1 %copy-start = (f32[18,4,1,8,256]{4,3,2,1,0:T(8,128)S(1)}, f32[18,4,1,8,256]{4,3,2,1,0:T(8,128)}, u32[]{:S(2)}) copy-start(f32[18,4,1,8,256]{4,3,2,1,0:T(8,128)} %rest.1) | copy-start | bytes 1769476
  1.7 0.9 %copy-start.1 = (f32[3,4,1,8,256]{4,3,2,1,0:T(8,128)S(1)}, f32[3,4,1,8,256]{4,3,2,1,0:T(8,128)}, u32[]{:S(2)}) copy-start(f32[3,4,1,8,256]{4,3,2,1,0:T(8,128)} %disp.1) | copy-start | bytes 294916
  2.6 0.9 %copy-start.2 = (f32[3,4,1,8,256]{4,3,2,1,0:T(8,128)S(1)}, f32[3,4,1,8,256]{4,3,2,1,0:T(8,128)}, u32[]{:S(2)}) copy-start(f32[3,4,1,8,256]{4,3,2,1,0:T(8,128)} %vel.1) | copy-start | bytes 294916
  3.5 0.7 %copy-start.3 = (s32[8,32]{1,0:T(8,128)S(1)}, s32[8,32]{1,0:T(8,128)}, u32[]{:S(2)}) copy-start(s32[8,32]{1,0:T(8,128)} %heights.1) | copy-start | bytes 3076

commit v2 on v1

--- a/solution.py
+++ b/solution.py
@@ -31,10 +31,17 @@
 ROUNDS = [(3, 0, 3), (1, 3, 3), (1, 4, 3), (1, 5, 1), (2, 6, 1)]
 
 
-def kernel(n_gx, n_yz, z_tiles, heights, disp, vel, rest, new_disp, new_vel, boost, *scratch):
+def kernel(n_gx, n_yz, z_tiles, heights_hbm, disp, rest_hbm, forces, boost, *scratch):
     xr, yr, zr, ys, zs = (scratch[i:25:5] for i in range(5))
-    (store, zb, hb, ins, bonds, part, first, sums, send_sem, recv_sem, red_send, red_recv) = scratch[25:]
+    (store, zb, hb, ins, bonds, part, first, sums, send_sem, recv_sem, red_send, red_recv, rest, heights, load_sem) = scratch[25:]
     nx_all, ny_all = heights.shape
+    loads = [
+        pltpu.make_async_copy(heights_hbm, heights, load_sem.at[0]),
+        pltpu.make_async_copy(disp.at[:, :, 0], xr[0].at[0], load_sem.at[1]),
+        pltpu.make_async_copy(rest_hbm, rest, load_sem.at[2]),
+    ]
+    for load in loads:
+        load.start()
     planes, rows, cols = disp.shape[1], disp.shape[3], disp.shape[4]
     y_tiles = n_yz // z_tiles
     gx = lax.axis_index("gx")
@@ -65,32 +72,59 @@
 
     lane = lax.broadcasted_iota(jnp.int32, (8, 128), 1)
 
+    left_slot = 1
+    right_slot = n_slots - 1
+    last_tile = z_tile == z_tiles - 1
+    first_tile = z_tile == 0
+
     def messages(r):
+        halo = ROUNDS[r][2]
         out = []
-        for ai, a in enumerate(x_steps):
-            if ai:
-                out.append((xr[r].at[0], xr[r].at[ai], a, 0, 0))
-        for bi in range(2):
-            for ai, a in enumerate(x_steps):
+        if halo == 1:
+            edge = planes - 1
+            out.append((xr[r].at[0, :, edge], xr[r].at[left_slot, :, edge], 1, 0, 0))
+            out.append((xr[r].at[0, :, 0], xr[r].at[right_slot, :, 0], -1, 0, 0))
+        else:
+            for ai in range(1, n_slots):
+                out.append((xr[r].at[0], xr[r].at[ai], x_steps[ai], 0, 0))
+        for ai, a in reversed(list(enumerate(x_steps))):
+            for bi in range(2):
                 out.append((ys[r].at[bi], yr[r].at[bi, ai], a, steps[1 + bi], 0))
         for ci in range(2):
-            for bi, b in enumerate(steps):
-                for ai, a in enumerate(x_steps):
-                    out.append((zs[r].at[ci], zr[r].at[ci, bi, ai], a, b, steps[1 + ci]))
+            for ai, a in enumerate(x_steps):
+                for bi in range(2):
+                    out.append((zs[r].at[ci, 1 - bi], zr[r].at[ci, ai, 2 + bi], a, steps[1 + bi], steps[1 + ci]))
+                out.append((zs[r].at[ci], zr[r].at[ci, ai, 0:2], a, 0, steps[1 + ci]))
         return [
-            pltpu.make_async_remote_copy(
-                src_ref=src,
-                dst_ref=dst,
-                send_sem=send_sem.at[r, i],
-                recv_sem=recv_sem.at[r, i],
-                device_id=target(a, b, c),
-                device_id_type=MESH,
+            (
+                c,
+                pltpu.make_async_remote_copy(
+                    src_ref=src,
+                    dst_ref=dst,
+                    send_sem=send_sem.at[r, i],
+                    recv_sem=recv_sem.at[r, i],
+                    device_id=target(a, b, c),
+                    device_id_type=MESH,
+                ),
             )
             for i, (src, dst, a, b, c) in enumerate(out)
         ]
 
+    def along(r, step, act, sending):
+        chosen = [copy for c, copy in messages(r) if c == step]
+        edge = last_tile if (step > 0) == sending else first_tile
+        if step == 0:
+            for copy in chosen:
+                act(copy)
+        else:
+
+            @pl.when(jnp.logical_not(edge))
+            def _():
+                for copy in chosen:
+                    act(copy)
+
     def pack(r):
-        count = ROUNDS[r][0]
+        count, _, halo = ROUNDS[r]
         up = jnp.zeros((8, 128), F32)
         down = jnp.zeros((8, 128), F32)
         for q in range(count):
@@ -101,27 +135,39 @@
                 here = (lane >= 4 * item) & (lane < 4 * item + 4)
                 up = jnp.where(here, pltpu.roll(high, (4 * item + 4) % 128, 1), up)
                 down = jnp.where(here, pltpu.roll(low, (4 * item) % 128, 1), down)
-                ys[r][0, q, p] = xr[r][0, q, p, rows - 4 : rows, :]
-                ys[r][1, q, p] = xr[r][0, q, p, 0:4, :]
-        zs[r][0] = up
-        zs[r][1] = down
+                for half in range(2):
+                    at = ((q * 2 + half) * planes + p) * halo
+                    span = slice(half * 128, half * 128 + 128)
+                    ys[r][0, at : at + halo] = xr[r][0, q, p, rows - halo : rows, span]
+                    ys[r][1, at : at + halo] = xr[r][0, q, p, 0:halo, span]
+        zs[r][0, 0], zs[r][0, 1] = up[0:4], up[4:8]
+        zs[r][1, 0], zs[r][1, 1] = down[0:4], down[4:8]
 
     def send(r):
-        pack(r)
-        for copy in messages(r):
-            copy.start()
+        if r:
+            pack(r)
+        for step in steps:
+            along(r, step, lambda copy: copy.start(), True)
 
     def receive(r):
-        for copy in messages(r):
-            copy.wait_recv()
+        for step in steps:
+            along(r, step, lambda copy: copy.wait_recv(), False)
         count, base, halo = ROUNDS[r]
-        for ai in range(n_slots):
-            for ci in range(2):
-                inside = z_tile > 0 if ci == 0 else z_tile < z_tiles - 1
-                keep = jnp.where(inside, 1.0, 0.0).astype(F32)
-                zb[ai, ci, 4:12] = zr[r][ci, 0, ai] * keep
-                zb[ai, ci, 0:4] = zr[r][ci, 1, ai, 4:8] * keep
-                zb[ai, ci, 12:16] = zr[r][ci, 2, ai, 0:4] * keep
+        for ci in range(2):
+            edge = first_tile if ci == 0 else last_tile
+
+            @pl.when(edge)
+            def _():
+                for ai in range(n_slots):
+                    zb[ai, ci] = jnp.zeros((16, 128), F32)
+
+            @pl.when(jnp.logical_not(edge))
+            def _():
+                for ai in range(n_slots):
+                    zb[ai, ci, 0:4] = zr[r][ci, ai, 2]
+                    zb[ai, ci, 4:8] = zr[r][ci, ai, 0]
+                    zb[ai, ci, 8:12] = zr[r][ci, ai, 1]
+                    zb[ai, ci, 12:16] = zr[r][ci, ai, 3]
 
         def one(xp, carry):
             plane = lax.rem(xp + 1, planes)
@@ -131,8 +177,9 @@
                 for half in range(2):
                     span = slice(half * 128, half * 128 + 128)
                     store[base + q, 3, half, xp, 4:12] = xr[r][slot, q, plane, :, span]
-                    store[base + q, 3, half, xp, 0:4] = yr[r][0, slot, q, plane, :, span]
-                    store[base + q, 3, half, xp, 12:16] = yr[r][1, slot, q, plane, :, span]
+                    at = ((q * 2 + half) * planes + plane) * halo
+                    store[base + q, 3, half, xp, 4 - halo : 4] = yr[r][0, slot, pl.ds(at, halo)]
+                    store[base + q, 3, half, xp, 12 : 12 + halo] = yr[r][1, slot, pl.ds(at, halo)]
             for q in range(count):
                 item = q * planes + plane
                 for rt in range(2):
@@ -185,9 +232,7 @@
 
         lax.fori_loop(0, 2 * planes, step, 0)
 
-    for q in range(3):
-        for p in range(planes):
-            xr[0][0, q, p] = disp[q, p, 0]
+    loads[0].wait()
 
     def height_row(xp, carry):
         at_x = lax.rem(gx * planes + xp - 3 + nx_all, nx_all)
@@ -197,8 +242,18 @@
         return carry
 
     lax.fori_loop(2, 4 + planes, height_row, 0)
+    loads[1].wait()
+    pack(0)
     pl.semaphore_wait(barrier, n_dev - 1)
     send(0)
+
+    def count_column(i, carry):
+        for j in range(ny_all):
+            carry = carry + jnp.clip(heights[i, j], 0, z_tiles * cols)
+        return carry
+
+    atoms = lax.fori_loop(0, nx_all, count_column, jnp.zeros((), jnp.int32))
+    loads[2].wait()
     receive(0)
 
     def bond_pass(i, x, half):
@@ -334,7 +389,6 @@
 
     tiles(adjoint_pull)
     receive(4)
-    receive(3)
 
     def final_pass(i, x, half):
         mine = [own(c, x, half) for c in range(3)]
@@ -351,34 +405,27 @@
             force = [force[c] + weight * s[c] for c in range(3)]
         span = pl.ds(pl.multiple_of(half * 128, 128), 128)
         for c in range(3):
-            speed = vel[c, x, 0, :, span] + 0.2 * force[c]
-            new_vel[c, x, 0, :, span] = speed
-            new_disp[c, x, 0, :, span] = mine[c] + 0.05 * speed
-
-    tiles(final_pass)
+            forces[c, x, 0, :, span] = force[c]
 
     def collect(k, carry):
         reduction(k).wait_recv()
         return carry
 
     lax.fori_loop(1, n_dev, collect, 0)
-    atoms = jnp.zeros((), jnp.int32)
-
-    def count_row(i, carry):
-        return carry + jnp.clip(heights[i // ny_all, lax.rem(i, ny_all)], 0, z_tiles * cols)
-
-    atoms = lax.fori_loop(0, nx_all * ny_all, count_row, atoms)
     total = jnp.sum(jnp.sum(sums[...], axis=0), axis=1, keepdims=True)
     boost[...] = jnp.broadcast_to(total, (1, 128)) / jnp.full((1, 128), atoms.astype(F32))
 
+    receive(3)
+    tiles(final_pass)
+
     def finish(k, carry):
         reduction(k).wait_send()
         return carry
 
     lax.fori_loop(1, n_dev, finish, 0)
     for r in range(5):
-        for copy in messages(r):
-            copy.wait_send()
+        for step in steps:
+            along(r, step, lambda copy: copy.wait_send(), True)
 
 
 def body(n_gx, n_yz, displacement, velocity, rest_length, heights):
@@ -386,15 +433,16 @@
     z_tiles = n_yz // (heights.shape[1] // rows)
     slots = 2 if n_gx == 2 else 3
     n_dev = n_gx * n_yz
-    n_msg = (slots - 1) + 2 * slots + 6 * slots
+    n_msg = 2 + 2 * slots + 6 * slots
     scratch = []
-    for count, _, _ in ROUNDS:
+    for count, _, halo in ROUNDS:
+        y_rows = count * 2 * planes * halo
         scratch += [
             pltpu.VMEM((slots, count, planes, rows, cols), F32),
-            pltpu.VMEM((2, slots, count, planes, 4, cols), F32),
-            pltpu.VMEM((2, 3, slots, 8, 128), F32),
-            pltpu.VMEM((2, count, planes, 4, cols), F32),
-            pltpu.VMEM((2, 8, 128), F32),
+            pltpu.VMEM((2, slots, y_rows, 128), F32),
+            pltpu.VMEM((2, slots, 4, 4, 128), F32),
+            pltpu.VMEM((2, y_rows, 128), F32),
+            pltpu.VMEM((2, 2, 4, 128), F32),
         ]
     scratch += [
         pltpu.VMEM((8, 7, 2, planes + 6, 16, 128), F32),
@@ -409,23 +457,27 @@
         pltpu.SemaphoreType.DMA((len(ROUNDS), n_msg)),
         pltpu.SemaphoreType.DMA((n_dev,)),
         pltpu.SemaphoreType.DMA((n_dev,)),
+        pltpu.VMEM(rest_length.shape, F32),
+        pltpu.SMEM(heights.shape, jnp.int32),
+        pltpu.SemaphoreType.DMA((3,)),
     ]
     vmem = pl.BlockSpec(memory_space=pltpu.VMEM)
-    new_disp, new_vel, boost = pl.pallas_call(
+    hbm = pl.BlockSpec(memory_space=pltpu.HBM)
+    forces, boost = pl.pallas_call(
         functools.partial(kernel, n_gx, n_yz, z_tiles),
         out_shape=(
             jax.ShapeDtypeStruct(displacement.shape, F32),
-            jax.ShapeDtypeStruct(velocity.shape, F32),
             jax.ShapeDtypeStruct((1, 128), F32),
         ),
-        in_specs=[pl.BlockSpec(memory_space=pltpu.SMEM), vmem, vmem, vmem],
-        out_specs=(vmem, vmem, vmem),
+        in_specs=[hbm, hbm, hbm],
+        out_specs=(vmem, vmem),
         scratch_shapes=scratch,
         compiler_params=pltpu.CompilerParams(
-            collective_id=0, has_side_effects=True, vmem_limit_bytes=48 * 1024 * 1024
+            collective_id=0, has_side_effects=True, vmem_limit_bytes=64_000_000
         ),
-    )(heights, displacement, velocity, rest_length)
-    return new_disp, new_vel, boost[0, 0]
+    )(heights, displacement, rest_length)
+    new_vel = velocity + 0.2 * forces
+    return displacement + 0.05 * new_vel, new_vel, boost[0, 0]
 
 
 def solution(mesh):

time: 55.6 us -> 44.4 us (0.80)
  Pallas kernels: 48.7 us -> 40.1 us
  local copies, waits for them, and re-layouts: 4.81 us -> 0.63 us
  other arithmetic: 0 us -> 1.59 us
    pallas_call x1, Pallas kernels: 48.7 us -> 40.1 us  [body(): pl.pallas_call(functools.partial(kernel, n_gx, n_yz, z_tiles), out_shape=...]
    unnamed x10 -> x6, local copies, waits for them, and re-layouts: 4.81 us -> 0.63 us
    add x0 -> x1, other arithmetic: none -> 1.59 us  [body(): return (displacement + 0.05 * new_vel, new_vel, boost[0, 0])]
where the time goes in v2:
time: 44.4 us; the launch traced here: 44.2 us
  Pallas kernels  40.1 us (90%)
  between operations  1.84 us (4%)
  other arithmetic  1.59 us (4%)
  local copies, waits for them, and re-layouts  0.63 us (1%)
    pallas_call x1, Pallas kernels, body(): pl.pallas_call(functools.partial(kernel, n_gx, n_yz, z_tiles), out_shape=...  40.1 us
    add x1, other arithmetic, body(): return (displacement + 0.05 * new_vel, new_vel, boost[0, 0])  1.59 us

profile of v2, /device:TPU:0, one launch (start us, length us, event | category | flops | bytes accessed | tf_op | source)
XLA Modules:
  0.0 44.2 jit_solution(17121219124775960292)
XLA Ops:
  0.6 0.0 copy-start
  0.6 0.0 copy-start.1
  0.7 40.1 %shard_map.67 = (f32[3,4,1,8,256]{4,3,2,1,0:T(8,128)}, f32[1,128]{1,0:T(1,128)}) custom-call(s32[8,32]{1,0:T(8,128)} %heights_hbm.1, f32[3,4,1,8,256]{4,3,2,1,0:T(8,128)} %disp.1, f32[18,4,1,8,256]{4,3,2,1,0:T(8,128)} %rest_hbm.1), custom_call_target="tpu_custom_call" | custom-call | tf_op jit(solution)/shard_map/pallas_call | solution.py:466
  40.8 0.0 copy-done
  40.8 0.0 copy-done.1
  40.8 1.6 %multiply_add_fusion = (f32[3,4,1,8,256]{4,3,2,1,0:T(8,128)}, f32[3,4,1,8,256]{4,3,2,1,0:T(8,128)}) fusion(f32[3,4,1,8,256]{4,3,2,1,0:T(8,128)S(1)} %copy-done, f32[3,4,1,8,256]{4,3,2,1,0:T(8,128)S(1)} %copy-done.1, f32[3,4,1,8,256]{4,3,2,1,0:T(8,128)} %get-tuple-element.5), kind=kLoop, calls=%fused_computation | loop fusion | flops 98304 | bytes 491520 | tf_op jit(solution)/shard_map/add | solution.py:480
  42.4 0.0 copy-start.2
  42.4 0.6 %copy-done.2 = f32[1,128]{1,0:T(1,128)S(1)} copy-done((f32[1,128]{1,0:T(1,128)S(1)}, f32[1,128]{1,0:T(1,128)}, u32[]{:S(2)}) %copy-start.2) | copy-done | bytes 536
Async XLA Ops:
  0.6 40.2 %copy-start = (f32[3,4,1,8,256]{4,3,2,1,0:T(8,128)S(1)}, f32[3,4,1,8,256]{4,3,2,1,0:T(8,128)}, u32[]{:S(2)}) copy-start(f32[3,4,1,8,256]{4,3,2,1,0:T(8,128)} %disp.1) | copy-start | bytes 294916
  0.6 40.2 %copy-start.1 = (f32[3,4,1,8,256]{4,3,2,1,0:T(8,128)S(1)}, f32[3,4,1,8,256]{4,3,2,1,0:T(8,128)}, u32[]{:S(2)}) copy-start(f32[3,4,1,8,256]{4,3,2,1,0:T(8,128)} %param.5) | copy-start | bytes 294916
  42.4 0.6 %copy-start.2 = (f32[1,128]{1,0:T(1,128)S(1)}, f32[1,128]{1,0:T(1,128)}, u32[]{:S(2)}) copy-start(f32[1,128]{1,0:T(1,128)} %get-tuple-element.6) | copy-start | bytes 1540

commit v3 on v2

--- a/solution.py
+++ b/solution.py
@@ -170,9 +170,8 @@
                     zb[ai, ci, 12:16] = zr[r][ci, ai, 3]
 
         def one(xp, carry):
-            plane = lax.rem(xp + 1, planes)
-            group = (xp + 1) // planes
-            slot = lax.rem(group + 1, 2) if n_gx == 2 else lax.rem(4 - group, 3)
+            plane = (xp - 3) % planes
+            slot = left_slot if xp < 3 else 0 if xp < 3 + planes else right_slot
             for q in range(count):
                 for half in range(2):
                     span = slice(half * 128, half * 128 + 128)
@@ -189,19 +188,20 @@
                     below = zb[slot, 0, band]
                     above = zb[slot, 1, band]
                     for dz in range(1, halo + 1):
-                        r0 = pltpu.roll(below, lax.rem(124 + 128 - 4 * item + dz, 128), 1)
+                        r0 = pltpu.roll(below, (124 - 4 * item + dz) % 128, 1)
                         r1 = pltpu.roll(t1, dz, 1)
                         r2 = pltpu.roll(t2, dz, 1)
                         store[base + q, 3 - dz, 0, xp, band] = jnp.where(lane < dz, r0, r1)
                         store[base + q, 3 - dz, 1, xp, band] = jnp.where(lane < dz, r1, r2)
                         s1 = pltpu.roll(t1, 128 - dz, 1)
                         s2 = pltpu.roll(t2, 128 - dz, 1)
-                        s3 = pltpu.roll(above, lax.rem(256 - 4 * item - dz, 128), 1)
+                        s3 = pltpu.roll(above, (-4 * item - dz) % 128, 1)
                         store[base + q, 3 + dz, 0, xp, band] = jnp.where(lane >= 128 - dz, s2, s1)
                         store[base + q, 3 + dz, 1, xp, band] = jnp.where(lane >= 128 - dz, s3, s2)
             return carry
 
-        lax.fori_loop(3 - halo, 3 + planes + halo, one, 0)
+        for xp in range(3 - halo, 3 + planes + halo):
+            one(xp, 0)
 
     def far(q, x, half, d):
         return store[q, d[2] + 3, half, x + 3 + d[0], 4 + d[1] : 12 + d[1]]
@@ -217,20 +217,15 @@
         return far(q, x, half, (0, 0, 0))
 
     def put(ref, q, x, half, value):
-        @pl.when(half == 0)
-        def _():
-            ref[0, q, x, :, 0:128] = value
-
-        @pl.when(half == 1)
-        def _():
-            ref[0, q, x, :, 128:256] = value
+        ref[0, q, x, :, half * 128 : half * 128 + 128] = value
 
     def tiles(body):
-        def step(i, carry):
-            body(i, i // 2, lax.rem(i, 2))
+        def step(x, carry):
+            for half in range(2):
+                body(2 * x + half, x, half)
             return carry
 
-        lax.fori_loop(0, 2 * planes, step, 0)
+        lax.fori_loop(0, planes, step, 0)
 
     loads[0].wait()
 
@@ -295,7 +290,7 @@
         part[i, 0] = room
 
     def rest_half(k, x, half):
-        return rest[k, x, 0, :, pl.ds(pl.multiple_of(half * 128, 128), 128)]
+        return rest[k, x, 0, :, slice(half * 128, half * 128 + 128)]
 
     tiles(bond_pass)
     send(1)
@@ -311,12 +306,16 @@
     receive(1)
     first[...] = jnp.zeros_like(first)
 
+    def tapered(q, i, x, half):
+        sums_of = [jnp.zeros((8, 128), F32) for _ in range(4)]
+        for k, d in enumerate(REACH):
+            inside = ins[i, k]
+            sums_of[k % 4] = sums_of[k % 4] + (inside * inside) * far(q, x, half, d)
+        return (sums_of[0] + sums_of[1]) + (sums_of[2] + sums_of[3])
+
     def smooth_pass(i, x, half):
         energy = own(3, x, half)
-        total = 1.0 + energy
-        for k, d in enumerate(REACH):
-            inside = ins[i, k]
-            total = total + (inside * inside) * far(3, x, half, d)
+        total = 1.0 + energy + tapered(3, i, x, half)
         room = part[i, 0]
         smooth = jnp.log(total) * 0.125
         share = 1.0 / (1.0 + smooth * smooth)
@@ -371,11 +370,7 @@
     receive(2)
 
     def lambda_pass(i, x, half):
-        total = own(4, x, half)
-        for k, d in enumerate(REACH):
-            inside = ins[i, k]
-            total = total + (inside * inside) * far(4, x, half, d)
-        put(xr[3], 0, x, half, total)
+        put(xr[3], 0, x, half, own(4, x, half) + tapered(4, i, x, half))
 
     tiles(lambda_pass)
     send(3)
@@ -403,7 +398,7 @@
                 - (gain + far(7, x, half, d)) * bonds[i, k, 3]
             )
             force = [force[c] + weight * s[c] for c in range(3)]
-        span = pl.ds(pl.multiple_of(half * 128, 128), 128)
+        span = slice(half * 128, half * 128 + 128)
         for c in range(3):
             forces[c, x, 0, :, span] = force[c]
 

time: 44.4 us -> 40.4 us (0.910)
  Pallas kernels: 40.1 us -> 36.1 us
    pallas_call x1, Pallas kernels: 40.1 us -> 36.1 us  [body(): pl.pallas_call(functools.partial(kernel, n_gx, n_yz, z_tiles), out_shape=...]
where the time goes in v3:
time: 40.4 us; the launch traced here: 40.2 us
  Pallas kernels  36.1 us (89%)
  between operations  1.84 us (5%)
  other arithmetic  1.59 us (4%)
  local copies, waits for them, and re-layouts  0.63 us (2%)
    pallas_call x1, Pallas kernels, body(): pl.pallas_call(functools.partial(kernel, n_gx, n_yz, z_tiles), out_shape=...  36.1 us
    add x1, other arithmetic, body(): return (displacement + 0.05 * new_vel, new_vel, boost[0, 0])  1.59 us

profile of v3, /device:TPU:0, one launch (start us, length us, event | category | flops | bytes accessed | tf_op | source)
XLA Modules:
  0.0 40.2 jit_solution(11551112802367816378)
XLA Ops:
  0.6 0.0 copy-start
  0.6 0.0 copy-start.1
  0.7 36.1 %shard_map.67 = (f32[3,4,1,8,256]{4,3,2,1,0:T(8,128)}, f32[1,128]{1,0:T(1,128)}) custom-call(s32[8,32]{1,0:T(8,128)} %heights_hbm.1, f32[3,4,1,8,256]{4,3,2,1,0:T(8,128)} %disp.1, f32[18,4,1,8,256]{4,3,2,1,0:T(8,128)} %rest_hbm.1), custom_call_target="tpu_custom_call" | custom-call | tf_op jit(solution)/shard_map/pallas_call | solution.py:461
  36.8 0.0 copy-done
  36.8 0.0 copy-done.1
  36.8 1.6 %multiply_add_fusion = (f32[3,4,1,8,256]{4,3,2,1,0:T(8,128)}, f32[3,4,1,8,256]{4,3,2,1,0:T(8,128)}) fusion(f32[3,4,1,8,256]{4,3,2,1,0:T(8,128)S(1)} %copy-done, f32[3,4,1,8,256]{4,3,2,1,0:T(8,128)S(1)} %copy-done.1, f32[3,4,1,8,256]{4,3,2,1,0:T(8,128)} %get-tuple-element.5), kind=kLoop, calls=%fused_computation | loop fusion | flops 98304 | bytes 491520 | tf_op jit(solution)/shard_map/add | solution.py:475
  38.4 0.0 copy-start.2
  38.4 0.6 %copy-done.2 = f32[1,128]{1,0:T(1,128)S(1)} copy-done((f32[1,128]{1,0:T(1,128)S(1)}, f32[1,128]{1,0:T(1,128)}, u32[]{:S(2)}) %copy-start.2) | copy-done | bytes 536
Async XLA Ops:
  0.6 36.2 %copy-start = (f32[3,4,1,8,256]{4,3,2,1,0:T(8,128)S(1)}, f32[3,4,1,8,256]{4,3,2,1,0:T(8,128)}, u32[]{:S(2)}) copy-start(f32[3,4,1,8,256]{4,3,2,1,0:T(8,128)} %disp.1) | copy-start | bytes 294916
  0.6 36.2 %copy-start.1 = (f32[3,4,1,8,256]{4,3,2,1,0:T(8,128)S(1)}, f32[3,4,1,8,256]{4,3,2,1,0:T(8,128)}, u32[]{:S(2)}) copy-start(f32[3,4,1,8,256]{4,3,2,1,0:T(8,128)} %param.5) | copy-start | bytes 294916
  38.4 0.6 %copy-start.2 = (f32[1,128]{1,0:T(1,128)S(1)}, f32[1,128]{1,0:T(1,128)}, u32[]{:S(2)}) copy-start(f32[1,128]{1,0:T(1,128)} %get-tuple-element.6) | copy-start | bytes 1540
